TPU v7x, 32 devices: a whole 2x2x4 slice. The times are simulated.
32 devices in a mesh: dp: 2 (over y), expert: 16 (over z, x, core).
Axes of the slice: x: 2, y: 2, z: 4, core: 2. Of those that a mesh axis runs over, the one named last changes fastest.
Arguments:
- out_grad: bfloat16 [768, 7168], P('expert', 'dp'), may hold values from -6 to 6
- gate_weight: float32 [768, 8], P('expert'), may hold values from 0.05 to 0.5
- expert_ids: int32 [768, 8], P('expert'), may hold values from 0 to 15, all different within a row; in each aligned block of 48 rows (0 to 47, 48 to 95, ...) at most 36 rows name the same one
- replicated: int32 [16], replicated, may hold values from 0 to 1, as said below
- down_weight: bfloat16 [16, 1024, 7168], P('expert', None, 'dp'), may hold values from -0.0625 to 0.0625
- pre_act: bfloat16 [16, 2, 576, 2048], P('expert', None, 'dp'), may hold values from -6 to 6
Outputs:
- grad_down: bfloat16 [16, 1024, 7168], P('expert', None, 'dp')
- grad_pre: bfloat16 [16, 2, 576, 2048], P('expert', None, 'dp')
Inputs may be any that keep to these rules, and one draw needn't show every extreme that they name: `expert_ids`: each row names 8 different experts; among the 48 rows of one device no expert is named more than 36 times, a bound that some block reaches. `replicated`: expert 0 always has a redundant slot; each other expert has one with chance one half.
All inputs are finite; a program needn't handle non-finite values.
Results may differ from a plain program's by a relative error of at most 0.018.
Values may be sent and summed in bfloat16 or wider, within the bound.
No kernel may reach another device: no remote copies, remote signals or barrier semaphores. Data moves between devices by JAX's collectives and lax.ppermute only.
A program may use at most 64 MiB of HBM per device.

v0:
```python
import jax
import jax.numpy as jnp
from jax import lax
from jax.sharding import PartitionSpec as P


def passed_along(value, axis, steps):
    count = lax.axis_size(axis)
    pairs = [(source, (source + steps) % count) for source in range(count)]
    return lax.ppermute(value, axis, pairs)


def hidden_of(stored):
    width = stored.shape[-1] // 2
    gate_part = stored[..., :width].astype(jnp.float32)
    up_part = stored[..., width:].astype(jnp.float32)
    return (gate_part * jax.nn.sigmoid(gate_part) * up_part).astype(jnp.bfloat16)


def swiglu_back(hidden_grad, stored):
    width = stored.shape[-1] // 2
    gate_part = stored[..., :width].astype(jnp.float32)
    up_part = stored[..., width:].astype(jnp.float32)
    sigmoid_v = jax.nn.sigmoid(gate_part)
    gate_grad = hidden_grad * up_part * sigmoid_v * (1.0 + gate_part * (1.0 - sigmoid_v))
    up_grad = hidden_grad * gate_part * sigmoid_v
    return jnp.concatenate([gate_grad, up_grad], axis=-1).astype(jnp.bfloat16)


def on_device(out_grad, gate_weight, expert_ids, replicated, down_weight, pre_act):
    devices = lax.axis_size("expert")
    half_way = devices // 2
    myself = lax.axis_index("expert")
    shares = lax.axis_size("dp")
    my_share = lax.axis_index("dp")
    tokens_here, choose = expert_ids.shape
    rows_share = pre_act.shape[2]
    all_rows = rows_share * shares
    capacity = all_rows // devices
    flat_ids = expert_ids.reshape(-1)
    experts_iota = jnp.arange(devices, dtype=jnp.int32)
    onehot = (flat_ids[:, None] == experts_iota[None, :]).astype(jnp.int32)
    position = jnp.sum(onehot * (jnp.cumsum(onehot, axis=0) - 1), axis=1)
    rep_of = jnp.sum(onehot * replicated[None, :], axis=1)
    diverted = (rep_of == 1) & (myself % 2 == 1)
    target_dev = jnp.where(diverted, (flat_ids + half_way) % devices, flat_ids)
    slot_index = diverted.astype(jnp.int32)
    target = slot_index * devices * capacity + target_dev * capacity + position
    placer = (
        jnp.arange(2 * devices * capacity, dtype=jnp.int32)[:, None] == target[None, :]
    ).astype(jnp.bfloat16)
    scaled = gate_weight[:, :, None] * out_grad.astype(jnp.float32)[:, None, :]
    routed = scaled.astype(jnp.bfloat16).reshape(tokens_here * choose, -1)
    outgoing = jnp.dot(placer, routed, preferred_element_type=jnp.float32).astype(jnp.bfloat16)
    outgoing = outgoing.reshape(2, devices, capacity, -1)
    arrived = lax.all_to_all(outgoing, "expert", split_axis=1, concat_axis=1, tiled=True).reshape(
        2, all_rows, -1
    )
    own_weight = down_weight[0]
    rep_self = jnp.sum(jnp.where(experts_iota == myself, replicated, 0))
    row_ids = my_share * rows_share + jnp.arange(rows_share, dtype=jnp.int32)
    taken_rows = (row_ids // capacity % 2 == 1) & (rep_self == 1)
    partner_rows, partner_pre = passed_along((arrived[1], pre_act[0, 1]), "expert", half_way)
    merged = arrived[0] + partner_rows
    merged_pre = jnp.where(taken_rows[:, None], partner_pre, pre_act[0, 0])
    partial_value = jnp.einsum("rd,fd->rf", merged, own_weight, preferred_element_type=jnp.float32)
    hidden = hidden_of(merged_pre)
    gradients = jnp.einsum(
        "rf,rd->fd",
        lax.all_gather(hidden, "dp", axis=0, tiled=True),
        merged,
        preferred_element_type=jnp.float32,
    )
    summed = lax.psum_scatter(
        partial_value.astype(jnp.bfloat16), "dp", scatter_dimension=0, tiled=True
    ).astype(jnp.float32)
    local_grad = swiglu_back(summed, merged_pre)
    blank_grad = jnp.zeros_like(local_grad)
    kept_grad = jnp.where(taken_rows[:, None], blank_grad, local_grad)
    sent_grad = jnp.where(taken_rows[:, None], local_grad, blank_grad)
    came_back = passed_along(sent_grad, "expert", half_way)
    grad_pre = jnp.stack([kept_grad, came_back])[None]
    grad_down = gradients.astype(jnp.bfloat16)[None]
    return (grad_down, grad_pre)


def solution(mesh):
    in_specs = (
        P("expert", "dp"),
        P("expert", None),
        P("expert", None),
        P(),
        P("expert", None, "dp"),
        P("expert", None, "dp", None),
    )
    out_specs = (P("expert", None, "dp"), P("expert", None, "dp", None))
    return jax.shard_map(
        on_device, mesh=mesh, in_specs=in_specs, out_specs=out_specs, check_vma=False
    )
```

profile of v0, /device:TPU:0, one launch (start us, length us, event | category | flops | bytes accessed | tf_op | source)
XLA Modules:
  0.0 598.2 jit_solution(13197197852552756951)
XLA Ops:
  7.2 0.0 reduce-scatter.2.cloned.1.call-start
  7.2 0.8 copy.12
  8.0 0.1 eq.79
  8.1 0.1 eq.86
  8.2 1.0 convert_element_type.49
  9.2 0.8 copy.15
  10.0 0.1 mul.75
  10.1 0.9 reduce-window.6
  10.9 0.2 slice_reduce_fusion.2
  11.2 0.8 select_reduce_fusion
  12.0 6.9 %convolution_convert_fusion = bf16[1152,3584]{1,0:T(8,128)(2,1)} fusion(f32[48,3584]{1,0:T(8,128)S(1)} %convert_element_type.49, f32[384]{0:T(512)S(1)} %mul.75, s32[384]{0:T(512)S(1)} %fusion.34), kind=kOutput, calls=%fused_computation | convolution fusion | flops 3178217472 | bytes 8948736 | tf_op jit(solution)/shard_map/dot_general | solution.py:54
  18.9 12.5 %reshape.148 = bf16[2,16,36,3584]{3,2,1,0:T(8,128)(2,1)} reshape(bf16[1152,3584]{1,0:T(8,128)(2,1)} %convolution_convert_fusion) | data formatting | bytes 16515072 | tf_op jit(solution)/shard_map/reshape | solution.py:55
  31.4 12.2 %copy.16 = bf16[2,16,36,3584]{3,0,2,1:T(2,128)(2,1)S(1)} copy(bf16[2,16,36,3584]{3,2,1,0:T(8,128)(2,1)} %reshape.148) | data formatting | bytes 16515072 | tf_op jit(solution)/shard_map/reshape | solution.py:55
  43.6 186.9 %all_to_all.5 = bf16[2,16,36,3584]{3,0,2,1:T(2,128)(2,1)S(1)} all-to-all(bf16[2,16,36,3584]{3,0,2,1:T(2,128)(2,1)S(1)} %copy.16), channel_id=1, replica_groups=mesh['dp'=2,'expert'=16] {'expert'}, dimensions={1} | all-to-all | bytes 16515072 | tf_op jit(solution)/shard_map/all_to_all | solution.py:56
  230.5 37.3 %slice_reduce_fusion = (bf16[16,36,3584]{2,1,0:T(8,128)(2,1)}, bf16[16,36,3584]{2,1,0:T(8,128)(2,1)}) fusion(bf16[2,16,36,3584]{3,0,2,1:T(2,128)(2,1)S(1)} %all_to_all.5), kind=kLoop, calls=%fused_computation.1 | loop fusion | bytes 16515072 | tf_op jit(solution)/shard_map/slice | solution.py:63
  267.8 6.9 %squeeze.18 = bf16[576,3584]{1,0:T(8,128)(2,1)} reshape(bf16[16,36,3584]{2,1,0:T(8,128)(2,1)} %get-tuple-element.2) | data formatting | bytes 8257536 | tf_op jit(solution)/shard_map/squeeze | solution.py:63
  274.7 2.7 collective-permute-start.1
  277.5 7.0 %squeeze.17 = bf16[576,3584]{1,0:T(8,128)(2,1)} reshape(bf16[16,36,3584]{2,1,0:T(8,128)(2,1)} %get-tuple-element.3) | data formatting | bytes 8257536 | tf_op jit(solution)/shard_map/squeeze | solution.py:64
  284.4 0.0 copy-start
  284.4 172.0 %collective-permute-done.1 = bf16[576,3584]{1,0:T(8,128)(2,1)} collective-permute-done((bf16[576,3584]{1,0:T(8,128)(2,1)}, bf16[576,3584]{1,0:T(8,128)(2,1)}, u32[]{:S(2)}, u32[]{:S(2)}) %collective-permute-start.1) | collective-permute-done | bytes 4128800 | tf_op jit(solution)/shard_map/ppermute | solution.py:10
  456.5 11.0 %fusion.9 = bf16[576,1024]{1,0:T(8,128)(2,1)} fusion(bf16[1,1024,3584]{2,1,0:T(8,128)(2,1)} %param.10, bf16[576,3584]{1,0:T(8,128)(2,1)} %squeeze.17, bf16[576,3584]{1,0:T(8,128)(2,1)} %collective-permute-done.1), kind=kOutput, calls=%fused_computation.19 | convolution fusion | flops 4230512640 | bytes 16777216 | tf_op jit(solution)/shard_map/rd,fd->rf/dot_general | solution.py:66
  467.5 0.0 copy-start.1
  467.5 0.0 reduce-scatter.2.cloned.1.call-update
  467.5 0.2 all-gather.2.cloned.1.call-start
  467.7 0.0 copy-done
  467.7 0.1 slice_bitcast_fusion
  467.9 0.1 collective-permute-start
  467.9 0.2 copy-done.1
  468.1 0.6 fusion.37
  469.4 52.0 %collective-permute-done = bf16[288,2048]{1,0:T(8,128)(2,1)S(1)} collective-permute-done((bf16[288,2048]{1,0:T(8,128)(2,1)S(1)}, bf16[288,2048]{1,0:T(8,128)(2,1)S(1)}, u32[]{:S(2)}, u32[]{:S(2)}) %collective-permute-start) | collective-permute-done | bytes 1179680 | tf_op jit(solution)/shard_map/ppermute | solution.py:10
  521.4 1.5 bitcast_select_fusion
  522.9 0.0 reduce-scatter.2.cloned.1.call-done
  522.9 2.7 fusion.17
  525.6 0.3 maximum_select_fusion.1
  525.9 0.1 collective-permute-start.2
  525.9 0.0 all-gather.2.cloned.1.call-update
  526.0 0.3 maximum_select_fusion
  526.2 53.0 %collective-permute-done.2 = bf16[288,2048]{1,0:T(8,128)(2,1)S(1)} collective-permute-done((bf16[288,2048]{1,0:T(8,128)(2,1)S(1)}, bf16[288,2048]{1,0:T(8,128)(2,1)S(1)}, u32[]{:S(2)}, u32[]{:S(2)}) %collective-permute-start.2) | collective-permute-done | bytes 1179680 | tf_op jit(solution)/shard_map/ppermute | solution.py:10
  579.2 1.6 maximum_bitcast_fusion
  580.8 0.0 all-gather.2.cloned.1.call-done
  580.8 10.5 %fusion.2 = bf16[1,1024,3584]{2,1,0:T(8,128)(2,1)} fusion(bf16[576,1024]{1,0:T(8,128)(2,1)} %all-gather.2.cloned.1.call-done, bf16[576,3584]{1,0:T(8,128)(2,1)} %squeeze.17, bf16[576,3584]{1,0:T(8,128)(2,1)} %collective-permute-done.1), kind=kOutput, calls=%fused_computation.6 | convolution fusion | flops 4233592832 | bytes 16777216 | tf_op jit(solution)/shard_map/rf,rd->fd/dot_general | solution.py:68
  (4 shorter events, 0.1 us)
Async XLA Ops:
  7.2 515.8 %reduce-scatter.2.cloned.1.call-start = ((), (), s32[]{:S(2)}) async-start(), calls=%async_computation.3 | async-start | bytes 1769472 | tf_op jit(solution)/shard_map/reduce_scatter | solution.py:74
  274.7 181.7 %collective-permute-start.1 = (bf16[576,3584]{1,0:T(8,128)(2,1)}, bf16[576,3584]{1,0:T(8,128)(2,1)}, u32[]{:S(2)}, u32[]{:S(2)}) collective-permute-start(bf16[576,3584]{1,0:T(8,128)(2,1)} %squeeze.18), channel_id=1, source_target_pairs={{0,8},{1,9},{2,10},{3,11},{4,12},{5,13},{6,14},{7,15},{8,0},{9,1},... | collective-permute-start | bytes 12386312 | tf_op jit(solution)/shard_map/ppermute | solution.py:10
  284.4 183.3 %copy-start = (bf16[1,2,288,2048]{3,2,1,0:T(8,128)(2,1)S(1)}, bf16[1,2,288,2048]{3,2,1,0:T(8,128)(2,1)}, u32[]{:S(2)}) copy-start(bf16[1,2,288,2048]{3,2,1,0:T(8,128)(2,1)} %param.11) | copy-start | bytes 7077892
  467.5 0.7 copy-start.1
  467.5 113.3 %all-gather.2.cloned.1.call-start = ((), (), s32[]{:S(2)}) async-start(), calls=%async_computation.2 | async-start | bytes 1769472 | tf_op jit(solution)/shard_map/all_gather | solution.py:70
  467.9 53.6 %collective-permute-start = (bf16[288,2048]{1,0:T(8,128)(2,1)S(1)}, bf16[288,2048]{1,0:T(8,128)(2,1)S(1)}, u32[]{:S(2)}, u32[]{:S(2)}) collective-permute-start(bf16[288,2048]{1,0:T(8,128)(2,1)S(1)} %slice_bitcast_fusion), channel_id=1, source_target_pairs={{0,8},{1,9},{2,10},{3,11},{4,12},{5,13},{6,14},{7,15},{8,0},{9,1},... | collective-permute-start | bytes 3538952 | tf_op jit(solution)/shard_map/ppermute | solution.py:10
  525.9 53.3 %collective-permute-start.2 = (bf16[288,2048]{1,0:T(8,128)(2,1)S(1)}, bf16[288,2048]{1,0:T(8,128)(2,1)S(1)}, u32[]{:S(2)}, u32[]{:S(2)}) collective-permute-start(bf16[288,2048]{1,0:T(8,128)(2,1)S(1)} %maximum_select_fusion.1), channel_id=1, source_target_pairs={{0,8},{1,9},{2,10},{3,11},{4,12},{5,13},{6,14},{7,15},{8,0},{9,1},... | collective-permute-start | bytes 3538952 | tf_op jit(solution)/shard_map/ppermute | solution.py:10
Sparse Core Ops, SparseCore 0:
  467.6 21.2 reduce-scatter.1
  526.1 23.0 all-gather.1
where the time goes:
time: 599 us; the launch traced here: 598 us
  waiting for transfers between devices  277 us (46%)
  blocking collectives  187 us (31%)
  local copies, waits for them, and re-layouts  78.3 us (13%)
  matrix products  28.4 us (5%)
  between operations  14.8 us (2%)
  other arithmetic  9.63 us (2%)
    ppermute x3, waiting for transfers between devices, passed_along(): return lax.ppermute(value, axis, pairs)  277 us
    all_to_all x1, blocking collectives, on_device(): lax.all_to_all(outgoing, 'expert', split_axis=1, concat_axis=1, tiled=True)  187 us
    slice x1, local copies, waits for them, and re-layouts, on_device(): arrived[1]  37.3 us
    reshape x2, local copies, waits for them, and re-layouts, on_device(): outgoing = outgoing.reshape(2, devices, capacity, -1)  24.8 us
  transfers between devices with their start and end apart: 5, of which 3 were waited for; matrix products, arithmetic and copies ran while one was open for 2% of the time, Pallas kernels for 0%

commit v1 on v0

--- a/solution.py
+++ b/solution.py
@@ -1,7 +1,20 @@
+import functools
+
 import jax
 import jax.numpy as jnp
 from jax import lax
+from jax.experimental import pallas as pl
+from jax.experimental.pallas import tpu as pltpu
 from jax.sharding import PartitionSpec as P
+
+
+LANES = 128
+FIELDS = 4
+
+
+def swapped(value, axis, mask):
+    count = lax.axis_size(axis)
+    return lax.ppermute(value, axis, [(s, s ^ mask) for s in range(count)])
 
 
 def passed_along(value, axis, steps):
@@ -27,7 +40,313 @@
     return jnp.concatenate([gate_grad, up_grad], axis=-1).astype(jnp.bfloat16)
 
 
-def on_device(out_grad, gate_weight, expert_ids, replicated, down_weight, pre_act):
+def in_vmem(body, outs, operands, scratch=(), copies=0, aliases=None, limit=8 << 20, hbm_in=(), hbm_out=()):
+    far = pl.BlockSpec(memory_space=pl.ANY)
+    whole = pl.BlockSpec(memory_space=pltpu.VMEM)
+    spaces = [far if i in hbm_in else whole for i in range(len(operands))]
+    operands = [
+        pltpu.with_memory_space_constraint(value, pltpu.HBM) if i in hbm_in else value
+        for i, value in enumerate(operands)
+    ]
+    return pl.pallas_call(
+        body,
+        in_specs=spaces,
+        out_specs=[far if i in hbm_out else whole for i in range(len(outs))],
+        out_shape=[
+            pltpu.HBM(shape, dtype) if i in hbm_out else jax.ShapeDtypeStruct(shape, dtype)
+            for i, (shape, dtype) in enumerate(outs)
+        ],
+        scratch_shapes=[pltpu.VMEM(shape, dtype) for shape, dtype in scratch]
+        + [pltpu.SemaphoreType.DMA((copies,))] * (copies > 0),
+        input_output_aliases=aliases or {},
+        compiler_params=pltpu.CompilerParams(vmem_limit_bytes=limit),
+    )(*operands)
+
+
+def payload_body(ids_hbm, weight_hbm, grad_hbm, out_ref, left_ref, right_ref, ids_ref, weight_ref, sems, *, experts):
+    tokens, width = grad_hbm.shape
+    half = width // 2
+    meta = out_ref.shape[1] - width
+    copies = [
+        pltpu.make_async_copy(source, target, sems.at[i])
+        for i, (source, target) in enumerate(
+            (
+                (ids_hbm, ids_ref),
+                (weight_hbm, weight_ref),
+                (grad_hbm, out_ref.at[:, pl.ds(0, width)]),
+                (grad_hbm.at[:, pl.ds(0, half)], left_ref.at[:, pl.ds(0, half)]),
+                (grad_hbm.at[:, pl.ds(half, half)], right_ref),
+            )
+        )
+    ]
+    for copy in copies:
+        copy.start()
+    lane = lax.broadcasted_iota(jnp.int32, (tokens, meta), 1)
+    expert, field = lane % experts, lane // experts
+    copies[0].wait()
+    copies[1].wait()
+    ids = jnp.transpose(ids_ref[...])
+    weight = jnp.transpose(weight_ref[...])
+    named = jnp.zeros((tokens, meta), jnp.float32)
+    chosen = jnp.zeros((tokens, meta), jnp.float32)
+    for k in range(ids.shape[1]):
+        hit = ids[:, k : k + 1] == expert
+        named = jnp.where(hit, 1.0, named)
+        chosen = jnp.where(hit, weight[:, k : k + 1], chosen)
+    rows = lax.broadcasted_iota(jnp.int32, (tokens, tokens), 0)
+    cols = lax.broadcasted_iota(jnp.int32, (tokens, tokens), 1)
+    earlier = (cols < rows).astype(jnp.bfloat16)
+    position = jnp.dot(earlier, named.astype(jnp.bfloat16), preferred_element_type=jnp.float32)
+    top = chosen.astype(jnp.bfloat16).astype(jnp.float32)
+    mid = (chosen - top).astype(jnp.bfloat16).astype(jnp.float32)
+    low = chosen - top - mid
+    place = jnp.where(named > 0.0, position, -1.0)
+    value = jnp.where(field == 0, place, jnp.where(field == 1, top, jnp.where(field == 2, mid, low)))
+    value = jnp.where(field < FIELDS, value, 0.0).astype(jnp.bfloat16)
+    out_ref[:, width:] = value
+    left_ref[:, half:] = value
+    for copy in copies[2:]:
+        copy.wait()
+
+
+def payload_of(out_grad, gate_weight, expert_ids, experts):
+    tokens, width = out_grad.shape
+    meta = -(-experts * FIELDS // LANES) * LANES
+    top = expert_ids.shape[1]
+    return in_vmem(
+        functools.partial(payload_body, experts=experts),
+        [((tokens, span), jnp.bfloat16) for span in (width + meta, width // 2 + meta, width // 2)],
+        [expert_ids.T, gate_weight.T, out_grad],
+        [((top, tokens), jnp.int32), ((top, tokens), jnp.float32)],
+        copies=5,
+        hbm_in=(0, 1, 2),
+    )
+
+
+def odd_first(rows, capacity):
+    parts = [rows[i * capacity : (i + 1) * capacity] for i in (1, 3, 0, 2)]
+    return jnp.concatenate(parts, axis=0)
+
+
+def chunk_body(*refs, experts, capacity, flip, halves, aliased, paired, parted):
+    shards, refs = refs[: 4 * halves], refs[4 * halves :]
+    weight = refs[0]
+    outs = refs[1 + aliased + paired :]
+    merged_ref, (stack_ref, pick_ref, value_ref) = outs[0], outs[-3:]
+    tokens = shards[0].shape[0]
+    _, width = weight.shape
+    meta = stack_ref.shape[1] - width
+    rows = 4 * capacity
+    myself = lax.axis_index("expert")
+    place = myself % 4
+    lane = lax.broadcasted_iota(jnp.int32, (tokens, meta), 1)
+    row = lax.broadcasted_iota(jnp.int32, (tokens, rows), 1)
+    for i, turn in enumerate((0, 2, 1, 3)):
+        span = slice(i * tokens, (i + 1) * tokens)
+        if halves == 1:
+            stack_ref[span, :] = shards[i][...]
+        else:
+            left, right = shards[i], shards[4 + i]
+            stack_ref[span, : width // 2] = left[:, : width // 2]
+            stack_ref[span, width // 2 : width] = right[...]
+            stack_ref[span, width:] = left[:, width // 2 :]
+        values = stack_ref[span, width:].astype(jnp.float32)
+        slot = jnp.sum(jnp.where(lane == myself, values, 0.0), axis=1, keepdims=True).astype(jnp.int32)
+        target = jnp.where(slot >= 0, slot + (place ^ turn) * capacity, -1)
+        pick_ref[span, :] = (target == row).astype(jnp.float32)
+    pick = pick_ref[...].T.astype(jnp.bfloat16)
+    chosen = jnp.dot(pick, stack_ref[...], preferred_element_type=jnp.float32)
+    lane = lax.broadcasted_iota(jnp.int32, (rows, meta), 1)
+    wanted = (lane % experts == myself) & (lane >= experts) & (lane < FIELDS * experts)
+    scale = jnp.sum(jnp.where(wanted, chosen[:, width:], 0.0), axis=1, keepdims=True)
+    merged = (scale * chosen[:, :width]).astype(jnp.bfloat16)
+    merged_ref[pl.ds(((myself // 4) ^ flip) * rows, rows), :] = merged
+    value = lax.dot_general(
+        weight[...], merged, (((1,), (1,)), ((), ())), preferred_element_type=jnp.float32
+    )
+    value_ref[...] = value.T
+    value = odd_first(value_ref, capacity).astype(jnp.bfloat16)
+    if not paired:
+        outs[1][...] = value
+        return
+    first = refs[1 + aliased]
+    owner = (myself // 8) == lax.axis_index("dp")
+    spans = [slice(0, rows // 2), slice(rows // 2, rows)] if parted else [slice(0, rows)]
+
+    @pl.when(owner)
+    def _():
+        for i, span in enumerate(spans):
+            outs[1 + i][...] = value[span]
+        outs[1 + len(spans)][...] = first[...]
+
+    @pl.when(jnp.logical_not(owner))
+    def _():
+        for i, span in enumerate(spans):
+            outs[1 + i][...] = first[span, :]
+        outs[1 + len(spans)][...] = value
+
+
+def chunk_of(shards, weight, merged, first, experts, capacity, all_rows, flip, parted):
+    tokens = shards[0].shape[0]
+    hidden, width = weight.shape
+    rows = 4 * capacity
+    meta = -(-experts * FIELDS // LANES) * LANES
+    aliased, paired = int(merged is not None), int(first is not None)
+    partial = [((rows, hidden), jnp.bfloat16)]
+    if paired:
+        partial = [((rows // 2, hidden), jnp.bfloat16)] * 2 + partial if parted else partial * 2
+    return in_vmem(
+        functools.partial(
+            chunk_body,
+            experts=experts,
+            capacity=capacity,
+            flip=flip,
+            halves=len(shards) // 4,
+            aliased=aliased,
+            paired=paired,
+            parted=parted,
+        ),
+        [((all_rows, width), jnp.bfloat16)] + partial,
+        [*shards, weight] + [merged] * aliased + [first] * paired,
+        [
+            ((4 * tokens, width + meta), jnp.bfloat16),
+            ((4 * tokens, rows), jnp.float32),
+            ((rows, hidden), jnp.float32),
+        ],
+        aliases={len(shards) + 1: 0} if aliased else None,
+        limit=14 << 20,
+    )
+
+
+BAND = 48
+
+
+def fetch_body(weight_hbm, stored_hbm, weight_ref, stored_ref, own_ref, far_ref, scratch_ref, sems, *, capacity):
+    copies = [
+        pltpu.make_async_copy(stored_hbm, stored_ref, sems.at[0]),
+        pltpu.make_async_copy(weight_hbm, weight_ref, sems.at[1]),
+    ]
+    for copy in copies:
+        copy.start()
+    copies[0].wait()
+    rows = stored_ref.shape[2]
+    for start in range(0, rows, BAND):
+        own_ref[start : start + BAND, :] = hidden_of(stored_ref[0, 0, start : start + BAND, :])
+        far = hidden_of(stored_ref[0, 1, start : start + BAND, :])
+        scratch_ref[start : start + BAND, :] = far.astype(jnp.float32)
+    odd = [
+        scratch_ref[start + capacity : start + 2 * capacity, :]
+        for start in range(0, rows, 2 * capacity)
+    ]
+    far_ref[...] = jnp.concatenate(odd, axis=0).astype(jnp.bfloat16)
+    copies[1].wait()
+
+
+def flag_of(flags_ref, expert):
+    flags = flags_ref[...]
+    lane = lax.broadcasted_iota(jnp.int32, flags.shape, 1)
+    return jnp.max(jnp.where(lane == expert, flags, 0), axis=1, keepdims=True) == 1
+
+
+def down_body(
+    flags_ref, mine_ref, other_ref, far_mine_ref, far_other_ref, merged_ref, out_hbm, rows_ref, turned_ref, out_ref, sems, *, capacity
+):
+    half, _ = mine_ref.shape
+    tile = out_ref.shape[2]
+    steps = merged_ref.shape[1] // tile
+    taken = flag_of(flags_ref, lax.axis_index("expert"))
+    share = lax.axis_index("dp")
+    for which in range(2):
+
+        @pl.when(share == which)
+        def _():
+            for i, (near, far) in enumerate(((mine_ref, far_mine_ref), (other_ref, far_other_ref))):
+                base = (which ^ i) * half
+                rows_ref[base : base + half, :] = near[...].astype(jnp.float32)
+                theirs = far[...].astype(jnp.float32)
+                for j in range(half // (2 * capacity)):
+                    start = base + (2 * j + 1) * capacity
+                    span = slice(start, start + capacity)
+                    moved = theirs[j * capacity : (j + 1) * capacity]
+                    rows_ref[span, :] = jnp.where(taken, moved, rows_ref[span, :])
+
+    turned_ref[...] = rows_ref[...].T.astype(jnp.bfloat16)
+    copies = []
+    for j in range(steps):
+        span = slice(j * tile, (j + 1) * tile)
+        if j > 1:
+            copies[j - 2].wait()
+        out_ref[j % 2] = jnp.dot(
+            turned_ref[...], merged_ref[:, span], preferred_element_type=jnp.float32
+        ).astype(jnp.bfloat16)
+        copies.append(
+            pltpu.make_async_copy(out_ref.at[j % 2], out_hbm.at[0, :, pl.ds(j * tile, tile)], sems.at[j % 2])
+        )
+        copies[j].start()
+    copies[-2].wait()
+    copies[-1].wait()
+
+
+def sum_body(flags_ref, kept_ref, came_ref, out_ref):
+    rows = out_ref.shape[0]
+    taken = flag_of(flags_ref, lax.axis_index("expert"))
+    value = kept_ref[:rows, :].astype(jnp.float32) + came_ref[:rows, :].astype(jnp.float32)
+    out_ref[...] = jnp.where(taken, value, 0.0).astype(jnp.bfloat16)
+
+
+def back_into(out_ref, value_ref, stored_ref, slot, base, rows):
+    for start in range(0, rows, BAND):
+        span = pl.ds(pl.multiple_of(base + start, 16), BAND)
+        out_ref[span, :] = swiglu_back(
+            value_ref[start : start + BAND, :], stored_ref[0, slot, span, :]
+        )
+
+
+def own_body(flags_ref, stored_ref, kept0, came0, kept1, odd1, even1, out_hbm, out_ref, value_ref, sems, *, capacity):
+    rows = 4 * capacity
+    myself = lax.axis_index("expert")
+    taken = flag_of(flags_ref, myself)
+    copies = []
+    for i, (kept, odd, even) in enumerate(
+        (
+            (kept0, came0[: rows // 2, :], came0[rows // 2 :, :]),
+            (kept1, odd1[...], even1[...]),
+        )
+    ):
+        base = (((myself // 4) & 1) ^ i) * rows
+        odds = kept[: rows // 2, :].astype(jnp.float32) + odd.astype(jnp.float32)
+        odds = jnp.where(taken, 0.0, odds)
+        evens = kept[rows // 2 :, :].astype(jnp.float32) + even.astype(jnp.float32)
+        for j in range(2):
+            span = slice(j * capacity, (j + 1) * capacity)
+            value_ref[2 * j * capacity : (2 * j + 1) * capacity, :] = evens[span]
+            value_ref[(2 * j + 1) * capacity : (2 * j + 2) * capacity, :] = odds[span]
+        back_into(out_ref, value_ref, stored_ref, 0, base, rows)
+        span = pl.ds(pl.multiple_of(base, 16), rows)
+        copies.append(pltpu.make_async_copy(out_ref.at[span], out_hbm.at[0, 0, span], sems.at[i]))
+        copies[i].start()
+    for copy in copies:
+        copy.wait()
+
+
+def far_body(stored_ref, came_ref, gradient_hbm, out_hbm, out_ref, value_ref, sems, *, capacity, pair):
+    rows = 4 * capacity
+    came = came_ref[...].astype(jnp.float32)
+    blank = jnp.zeros((capacity, came.shape[1]), jnp.float32)
+    for j in range(2):
+        value_ref[2 * j * capacity : (2 * j + 1) * capacity, :] = blank
+        value_ref[(2 * j + 1) * capacity : (2 * j + 2) * capacity, :] = came[
+            j * capacity : (j + 1) * capacity
+        ]
+    base = (((lax.axis_index("expert") // 4) & 1) ^ pair) * rows
+    back_into(out_ref, value_ref, stored_ref, 1, base, rows)
+    span = pl.ds(pl.multiple_of(base, 16), rows)
+    copy = pltpu.make_async_copy(out_ref.at[span], out_hbm.at[0, 1, span], sems.at[0])
+    copy.start()
+    copy.wait()
+
+
+def on_any_mesh(out_grad, gate_weight, expert_ids, replicated, down_weight, pre_act):
     devices = lax.axis_size("expert")
     half_way = devices // 2
     myself = lax.axis_index("expert")
@@ -84,6 +403,100 @@
     return (grad_down, grad_pre)
 
 
+def on_device(out_grad, gate_weight, expert_ids, replicated, down_weight, pre_act):
+    devices = lax.axis_size("expert")
+    half_way = devices // 2
+    rows_share, wide = pre_act.shape[2:]
+    all_rows = rows_share * lax.axis_size("dp")
+    capacity = all_rows // devices
+    hidden_width, width = down_weight.shape[1:]
+    flags = replicated[None]
+    bfloat = jnp.bfloat16
+    single = jnp.float32
+
+    payload, left, right = payload_of(out_grad, gate_weight, expert_ids, devices)
+    column = {"0": payload}
+    for name, base, bits in (("1", payload, 1), ("2L", left, 2), ("2R", right, 2)):
+        column[name] = swapped(base, "expert", 4 * bits)
+    for part in "LR":
+        column["3" + part] = swapped(column["2" + part], "expert", 4)
+    across, beside, corner = {}, {}, {}
+    for name in column:
+        across[name] = swapped(column[name], "expert", 2)
+        beside[name] = swapped(column[name], "expert", 1)
+        corner[name] = swapped(across[name], "expert", 1)
+
+    own_weight, stored, own_hidden, far_hidden = in_vmem(
+        functools.partial(fetch_body, capacity=capacity),
+        [
+            ((hidden_width, width), bfloat),
+            (pre_act.shape, bfloat),
+            ((rows_share, wide // 2), bfloat),
+            ((rows_share // 2, wide // 2), bfloat),
+        ],
+        [down_weight[0], pre_act],
+        [((rows_share, wide // 2), single)],
+        copies=2,
+        hbm_in=(0, 1),
+    )
+    other_hidden = swapped(own_hidden, "dp", 1)
+    far_mine = passed_along(far_hidden, "expert", half_way)
+    far_other = swapped(far_mine, "dp", 1)
+
+    def chunk(k, names, merged, first, parted=False):
+        shards = [group[name] for name in names for group in (column, across, beside, corner)]
+        return chunk_of(
+            shards, own_weight, merged, first, devices, capacity, all_rows, k, parted
+        )
+
+    merged, first0 = chunk(0, ("0",), None, None)
+    merged, first1 = chunk(1, ("1",), merged, None)
+    merged, sent0, kept0 = chunk(2, ("2L", "2R"), merged, first0)
+    merged, odd1, even1, kept1 = chunk(3, ("3L", "3R"), merged, first1, parted=True)
+    came = {}
+    for name, value in (("r0", sent0), ("r1o", odd1), ("r1e", even1)):
+        came[name] = swapped(value, "dp", 1)
+    back = []
+    for kept, arrived in ((kept0, came["r0"]), (kept1, came["r1o"])):
+        outgoing = in_vmem(sum_body, [((2 * capacity, hidden_width), bfloat)], [flags, kept, arrived])[0]
+        back.append(passed_along(outgoing, "expert", half_way))
+
+    tile = 512
+    gradients = in_vmem(
+        functools.partial(down_body, capacity=capacity),
+        [((1, hidden_width, width), bfloat)],
+        [flags, own_hidden, other_hidden, far_mine, far_other, merged],
+        [
+            ((all_rows, hidden_width), single),
+            ((hidden_width, all_rows), bfloat),
+            ((2, hidden_width, tile), bfloat),
+        ],
+        copies=2,
+        hbm_out=(0,),
+        limit=14 << 20,
+    )[0]
+    grad_pre = in_vmem(
+        functools.partial(own_body, capacity=capacity),
+        [(pre_act.shape, bfloat)],
+        [flags, stored, kept0, came["r0"], kept1, came["r1o"], came["r1e"]],
+        [((rows_share, wide), bfloat), ((4 * capacity, wide // 2), single)],
+        copies=2,
+        hbm_out=(0,),
+    )[0]
+    for i in range(2):
+        grad_pre = in_vmem(
+            functools.partial(far_body, capacity=capacity, pair=i),
+            [(pre_act.shape, bfloat)],
+            [stored, back[i], grad_pre],
+            [((rows_share, wide), bfloat), ((4 * capacity, wide // 2), single)],
+            copies=1,
+            aliases={2: 0},
+            hbm_in=(2,),
+            hbm_out=(0,),
+        )[0]
+    return (gradients, grad_pre)
+
+
 def solution(mesh):
     in_specs = (
         P("expert", "dp"),
@@ -94,6 +507,11 @@
         P("expert", None, "dp", None),
     )
     out_specs = (P("expert", None, "dp"), P("expert", None, "dp", None))
+    fits = mesh.shape["dp"] == 2 and mesh.shape["expert"] == 16
     return jax.shard_map(
-        on_device, mesh=mesh, in_specs=in_specs, out_specs=out_specs, check_vma=False
-    )
+        on_device if fits else on_any_mesh,
+        mesh=mesh,
+        in_specs=in_specs,
+        out_specs=out_specs,
+        check_vma=False,
+    )

time: 599 us -> 112 us (0.19)
  waiting for transfers between devices: 277 us -> 46.4 us
  blocking collectives: 187 us -> 0 us
  local copies, waits for them, and re-layouts: 78.3 us -> 0.01 us
  starting transfers between devices: 3.12 us -> 33.9 us
  Pallas kernels: 0 us -> 30 us
  matrix products: 28.4 us -> 0 us
  between operations: 14.8 us -> 0.93 us
  other arithmetic: 9.63 us -> 0 us
    ppermute x3, waiting for transfers between devices: 277 us -> 0.01 us  [passed_along(): return lax.ppermute(value, axis, pairs)]
    all_to_all x1 -> x0, blocking collectives: 187 us -> none  [on_device(): lax.all_to_all(outgoing, 'expert', split_axis=1, concat_axis=1, tiled=True)]
    ppermute x0 -> x28, waiting for transfers between devices: none -> 46.4 us  [swapped(): return lax.ppermute(value, axis, [(s, s ^ mask) for s in range(count)])]
    slice x2 -> x0, local copies, waits for them, and re-layouts: 37.5 us -> none  [the longest x1 37.3 us: on_device(): arrived[1]]
    pallas_call x0 -> x12, Pallas kernels: none -> 30 us  [in_vmem(): pl.pallas_call(body, in_specs=spaces, out_specs=[far if i in hbm_out else...]
    dot_general x3 -> x0, matrix products: 28.4 us -> none  [the longest x1 11 us: on_device(): jnp.einsum('rd,fd->rf', merged, own_weight, preferred_element_type=jnp.fl...]
    reshape x2 -> x0, local copies, waits for them, and re-layouts: 24.8 us -> none  [on_device(): outgoing = outgoing.reshape(2, devices, capacity, -1)]
    ppermute x0 -> x28, starting transfers between devices: none -> 22.9 us  [swapped(): return lax.ppermute(value, axis, [(s, s ^ mask) for s in range(count)])]
  transfers between devices with their start and end apart: 5 -> 31, of which waited for: 3 -> 9; matrix products, arithmetic and copies ran while one was open for 2% -> 0% of each run, Pallas kernels for 0% -> 22%
where the time goes in v1:
time: 112 us; the launch traced here: 111 us
  waiting for transfers between devices  46.4 us (41%)
  starting transfers between devices  33.9 us (30%)
  Pallas kernels  30 us (27%)
    ppermute x28, waiting for transfers between devices, swapped(): return lax.ppermute(value, axis, [(s, s ^ mask) for s in range(count)])  46.4 us
    pallas_call x12, Pallas kernels, in_vmem(): pl.pallas_call(body, in_specs=spaces, out_specs=[far if i in hbm_out else...  30 us
    ppermute x28, starting transfers between devices, swapped(): return lax.ppermute(value, axis, [(s, s ^ mask) for s in range(count)])  22.9 us
    ppermute x3, starting transfers between devices, passed_along(): return lax.ppermute(value, axis, pairs)  11 us
  transfers between devices with their start and end apart: 31, of which 9 were waited for; matrix products, arithmetic and copies ran while one was open for 0% of the time, Pallas kernels for 22%

profile of v1, /device:TPU:0, one launch (start us, length us, event | category | flops | bytes accessed | tf_op | source)
XLA Modules:
  0.0 111.3 jit_solution(4085496744452581542)
XLA Ops:
  0.6 3.8 %shard_map.77 = (bf16[1024,3584]{1,0:T(8,128)(2,1)S(1)}, bf16[1,2,288,2048]{3,2,1,0:T(8,128)(2,1)S(1)}, bf16[288,1024]{1,0:T(8,128)(2,1)S(1)}, bf16[144,1024]{1,0:T(8,128)(2,1)S(1)}) custom-call(bf16[1024,3584]{1,0:T(8,128)(2,1)} %bitcast.8, bf16[1,2,288,2048]{3,2,1,0:T(8,128)(2,1)} %stored_hbm.1), custom_call_target="tpu_custom_call" | custom-call | tf_op jit(solution)/shard_map/pallas_call | solution.py:51
  4.5 4.1 %collective-permute-start.1 = (bf16[144,1024]{1,0:T(8,128)(2,1)S(1)}, bf16[144,1024]{1,0:T(8,128)(2,1)S(1)}, u32[]{:S(2)}, u32[]{:S(2)}) collective-permute-start(bf16[144,1024]{1,0:T(8,128)(2,1)S(1)} %get-tuple-element.21), channel_id=1, source_target_pairs={{0,8},{1,9},{2,10},{3,11},{4,12},{5,13},{6,14},{7,15},{8,0},{9,1},... | collective-permute-start | bytes 884744 | tf_op jit(solution)/shard_map/ppermute | solution.py:23
  8.6 1.2 %shard_map.78 = (bf16[48,3712]{1,0:T(8,128)(2,1)S(1)}, bf16[48,1920]{1,0:T(8,128)(2,1)S(1)}, bf16[48,1792]{1,0:T(8,128)(2,1)S(1)}) custom-call(s32[8,48]{1,0:T(8,128)} %bitcast.9, f32[8,48]{1,0:T(8,128)} %bitcast.10, bf16[48,3584]{1,0:T(8,128)(2,1)} %grad_hbm.1), custom_call_target="tpu_custom_call" | custom-call | tf_op jit(solution)/shard_map/pallas_call | solution.py:51
  9.8 0.1 collective-permute-start.8
  9.9 1.9 %collective-permute-start.19 = (bf16[48,3712]{1,0:T(8,128)(2,1)S(1)}, bf16[48,3712]{1,0:T(8,128)(2,1)S(1)}, u32[]{:S(2)}, u32[]{:S(2)}) collective-permute-start(bf16[48,3712]{1,0:T(8,128)(2,1)S(1)} %get-tuple-element.25.refs_0_), channel_id=1, source_target_pairs={{0,4},{1,5},{2,6},{3,7},{4,0},{5,1},{6,2},{7,3},{8,12},{9,13},{10,... | collective-permute-start | bytes 1069064 | tf_op jit(solution)/shard_map/ppermute | solution.py:17
  11.8 2.6 %collective-permute-start.3 = (bf16[48,1920]{1,0:T(8,128)(2,1)S(1)}, bf16[48,1920]{1,0:T(8,128)(2,1)S(1)}, u32[]{:S(2)}, u32[]{:S(2)}) collective-permute-start(bf16[48,1920]{1,0:T(8,128)(2,1)S(1)} %get-tuple-element.22), channel_id=1, source_target_pairs={{0,8},{1,9},{2,10},{3,11},{4,12},{5,13},{6,14},{7,15},{8,0},{9,1},... | collective-permute-start | bytes 552968 | tf_op jit(solution)/shard_map/ppermute | solution.py:17
  14.4 1.5 %collective-permute-start.23 = (bf16[48,3712]{1,0:T(8,128)(2,1)S(1)}, bf16[48,3712]{1,0:T(8,128)(2,1)S(1)}, u32[]{:S(2)}, u32[]{:S(2)}) collective-permute-start(bf16[48,3712]{1,0:T(8,128)(2,1)S(1)} %get-tuple-element.25.refs_0_), channel_id=1, source_target_pairs={{0,2},{1,3},{2,0},{3,1},{4,6},{5,7},{6,4},{7,5},{8,10},{9,11},{10,... | collective-permute-start | bytes 1069064 | tf_op jit(solution)/shard_map/ppermute | solution.py:17
  15.8 18.2 %collective-permute-done.8.refs_4_ = bf16[48,1792]{1,0:T(8,128)(2,1)S(1)} collective-permute-done((bf16[48,1792]{1,0:T(8,128)(2,1)S(1)}, bf16[48,1792]{1,0:T(8,128)(2,1)S(1)}, u32[]{:S(2)}, u32[]{:S(2)}) %collective-permute-start.8) | collective-permute-done | bytes 172064 | tf_op jit(solution)/shard_map/ppermute | solution.py:17
  34.1 1.8 %collective-permute-start.16 = (bf16[48,1792]{1,0:T(8,128)(2,1)S(1)}, bf16[48,1792]{1,0:T(8,128)(2,1)S(1)}, u32[]{:S(2)}, u32[]{:S(2)}) collective-permute-start(bf16[48,1792]{1,0:T(8,128)(2,1)S(1)} %collective-permute-done.8.refs_4_), channel_id=1, source_target_pairs={{0,2},{1,3},{2,0},{3,1},{4,6},{5,7},{6,4},{7,5},{8,10},{9,11},{10,... | collective-permute-start | bytes 516104 | tf_op jit(solution)/shard_map/ppermute | solution.py:17
  35.9 1.3 %collective-permute-done.3.refs_0_ = bf16[48,1920]{1,0:T(8,128)(2,1)S(1)} collective-permute-done((bf16[48,1920]{1,0:T(8,128)(2,1)S(1)}, bf16[48,1920]{1,0:T(8,128)(2,1)S(1)}, u32[]{:S(2)}, u32[]{:S(2)}) %collective-permute-start.3) | collective-permute-done | bytes 184352 | tf_op jit(solution)/shard_map/ppermute | solution.py:17
  37.2 0.0 collective-permute-start.24
  37.2 0.0 collective-permute-done.1.far_mine_ref
  37.2 0.5 collective-permute-start.17
  37.7 1.8 %collective-permute-done.16.refs_5_ = bf16[48,1792]{1,0:T(8,128)(2,1)S(1)} collective-permute-done((bf16[48,1792]{1,0:T(8,128)(2,1)S(1)}, bf16[48,1792]{1,0:T(8,128)(2,1)S(1)}, u32[]{:S(2)}, u32[]{:S(2)}) %collective-permute-start.16) | collective-permute-done | bytes 172064 | tf_op jit(solution)/shard_map/ppermute | solution.py:17
  39.5 0.8 collective-permute-start.9
  40.3 0.0 collective-permute-done.19.refs_0_
  40.3 1.5 %collective-permute-start.20 = (bf16[48,3712]{1,0:T(8,128)(2,1)S(1)}, bf16[48,3712]{1,0:T(8,128)(2,1)S(1)}, u32[]{:S(2)}, u32[]{:S(2)}) collective-permute-start(bf16[48,3712]{1,0:T(8,128)(2,1)S(1)} %collective-permute-done.19.refs_0_), channel_id=1, source_target_pairs={{0,2},{1,3},{2,0},{3,1},{4,6},{5,7},{6,4},{7,5},{8,10},{9,11},{10,... | collective-permute-start | bytes 1069064 | tf_op jit(solution)/shard_map/ppermute | solution.py:17
  41.8 0.0 collective-permute-done.17.refs_6_
  41.8 0.5 collective-permute-start.13
  42.3 2.6 %collective-permute-done.9.refs_4_ = bf16[48,1792]{1,0:T(8,128)(2,1)S(1)} collective-permute-done((bf16[48,1792]{1,0:T(8,128)(2,1)S(1)}, bf16[48,1792]{1,0:T(8,128)(2,1)S(1)}, u32[]{:S(2)}, u32[]{:S(2)}) %collective-permute-start.9) | collective-permute-done | bytes 172064 | tf_op jit(solution)/shard_map/ppermute | solution.py:17
  44.9 0.0 collective-permute-start.14
  44.9 0.0 collective-permute-done.23.refs_1_
  44.9 0.8 collective-permute-start.4
  45.7 0.0 collective-permute-done.24.refs_2_
  45.7 0.2 collective-permute-start.18
  46.0 7.3 %collective-permute-done.13.refs_1_ = bf16[48,1920]{1,0:T(8,128)(2,1)S(1)} collective-permute-done((bf16[48,1920]{1,0:T(8,128)(2,1)S(1)}, bf16[48,1920]{1,0:T(8,128)(2,1)S(1)}, u32[]{:S(2)}, u32[]{:S(2)}) %collective-permute-start.13) | collective-permute-done | bytes 184352 | tf_op jit(solution)/shard_map/ppermute | solution.py:17
  53.3 1.5 %collective-permute-start.10 = (bf16[48,1792]{1,0:T(8,128)(2,1)S(1)}, bf16[48,1792]{1,0:T(8,128)(2,1)S(1)}, u32[]{:S(2)}, u32[]{:S(2)}) collective-permute-start(bf16[48,1792]{1,0:T(8,128)(2,1)S(1)} %collective-permute-done.9.refs_4_), channel_id=1, source_target_pairs={{0,2},{1,3},{2,0},{3,1},{4,6},{5,7},{6,4},{7,5},{8,10},{9,11},{10,... | collective-permute-start | bytes 516104 | tf_op jit(solution)/shard_map/ppermute | solution.py:17
  54.8 0.5 collective-permute-start.21
  55.3 0.1 collective-permute-start.22
  55.4 0.0 collective-permute-done.18.refs_7_
  55.4 0.4 collective-permute-start.15
  55.8 3.1 %collective-permute-done.10.refs_5_ = bf16[48,1792]{1,0:T(8,128)(2,1)S(1)} collective-permute-done((bf16[48,1792]{1,0:T(8,128)(2,1)S(1)}, bf16[48,1792]{1,0:T(8,128)(2,1)S(1)}, u32[]{:S(2)}, u32[]{:S(2)}) %collective-permute-start.10) | collective-permute-done | bytes 172064 | tf_op jit(solution)/shard_map/ppermute | solution.py:17
  58.9 1.9 %collective-permute-start.5 = (bf16[48,1920]{1,0:T(8,128)(2,1)S(1)}, bf16[48,1920]{1,0:T(8,128)(2,1)S(1)}, u32[]{:S(2)}, u32[]{:S(2)}) collective-permute-start(bf16[48,1920]{1,0:T(8,128)(2,1)S(1)} %collective-permute-done.4.refs_0_), channel_id=1, source_target_pairs={{0,2},{1,3},{2,0},{3,1},{4,6},{5,7},{6,4},{7,5},{8,10},{9,11},{10,... | collective-permute-start | bytes 552968 | tf_op jit(solution)/shard_map/ppermute | solution.py:17
  60.8 0.0 collective-permute-done.15.refs_3_
  60.8 0.0 collective-permute-start.11
  60.8 3.6 %collective-permute-done.5.refs_1_ = bf16[48,1920]{1,0:T(8,128)(2,1)S(1)} collective-permute-done((bf16[48,1920]{1,0:T(8,128)(2,1)S(1)}, bf16[48,1920]{1,0:T(8,128)(2,1)S(1)}, u32[]{:S(2)}, u32[]{:S(2)}) %collective-permute-start.5) | collective-permute-done | bytes 184352 | tf_op jit(solution)/shard_map/ppermute | solution.py:17
  64.4 1.5 %collective-permute-start = (bf16[288,1024]{1,0:T(8,128)(2,1)S(1)}, bf16[288,1024]{1,0:T(8,128)(2,1)S(1)}, u32[]{:S(2)}, u32[]{:S(2)}) collective-permute-start(bf16[288,1024]{1,0:T(8,128)(2,1)S(1)} %get-tuple-element.20.mine_ref), channel_id=1, source_target_pairs={{0,16},{16,0},{1,17},{17,1},{2,18},{18,2},{3,19},{19,3},{4,20},{20... | collective-permute-start | bytes 1769480 | tf_op jit(solution)/shard_map/ppermute | solution.py:17
  66.0 0.0 collective-permute-done.21.refs_2_
  66.0 0.5 collective-permute-start.7
  66.5 0.1 collective-permute-start.12
  66.5 2.9 %shard_map.79 = (bf16[576,3584]{1,0:T(8,128)(2,1)S(1)}, bf16[144,1024]{1,0:T(8,128)(2,1)S(1)}) custom-call(bf16[48,3712]{1,0:T(8,128)(2,1)S(1)} %get-tuple-element.25.refs_0_, bf16[48,3712]{1,0:T(8,128)(2,1)S(1)} %collective-permute-done.23.refs_1_, bf16[48,3712]{1,0:T(8,128)(2,1)S(1)} %collective-permute-done.24.refs_2_, ...), custom_call_target="tpu_custom_call" | custom-call | tf_op jit(solution)/shard_map/pallas_call | solution.py:51
  69.4 2.9 %shard_map.80 = (bf16[576,3584]{1,0:T(8,128)(2,1)S(1)}, bf16[144,1024]{1,0:T(8,128)(2,1)S(1)}) custom-call(bf16[48,3712]{1,0:T(8,128)(2,1)S(1)} %collective-permute-done.19.refs_0_, bf16[48,3712]{1,0:T(8,128)(2,1)S(1)} %collective-permute-done.20.refs_1_, bf16[48,3712]{1,0:T(8,128)(2,1)S(1)} %collective-permute-done.21.refs_2_, ...), custom_call_target="tpu_custom_call", output_to_operand_aliasing={{0}: (5, {})} | custom-call | tf_op jit(solution)/shard_map/pallas_call | solution.py:51
  72.3 2.9 %shard_map.81 = (bf16[576,3584]{1,0:T(8,128)(2,1)S(1)}, bf16[144,1024]{1,0:T(8,128)(2,1)S(1)}, bf16[144,1024]{1,0:T(8,128)(2,1)S(1)}) custom-call(bf16[48,1920]{1,0:T(8,128)(2,1)S(1)} %collective-permute-done.3.refs_0_, bf16[48,1920]{1,0:T(8,128)(2,1)S(1)} %collective-permute-done.13.refs_1_, ...), custom_call_target="tpu_custom_call", output_to_operand_aliasing={{0}: (9, {})} | custom-call | tf_op jit(solution)/shard_map/pallas_call | solution.py:51
  75.3 0.0 collective-permute-done.11.refs_6_
  75.3 0.6 collective-permute-start.28
  75.8 0.0 collective-permute-done.6.refs_2_
  75.8 1.5 %collective-permute-start.2 = (bf16[144,1024]{1,0:T(8,128)(2,1)S(1)}, bf16[144,1024]{1,0:T(8,128)(2,1)S(1)}, u32[]{:S(2)}, u32[]{:S(2)}) collective-permute-start(bf16[144,1024]{1,0:T(8,128)(2,1)S(1)} %collective-permute-done.1.far_mine_ref), channel_id=1, source_target_pairs={{0,16},{16,0},{1,17},{17,1},{2,18},{18,2},{3,19},{19,3},{4,20},{20... | collective-permute-start | bytes 884744 | tf_op jit(solution)/shard_map/ppermute | solution.py:17
  77.4 3.1 %shard_map.82 = (bf16[576,3584]{1,0:T(8,128)(2,1)S(1)}, bf16[72,1024]{1,0:T(8,128)(2,1)S(1)}, bf16[72,1024]{1,0:T(8,128)(2,1)S(1)}, bf16[144,1024]{1,0:T(8,128)(2,1)S(1)}) custom-call(bf16[48,1920]{1,0:T(8,128)(2,1)S(1)} %collective-permute-done.4.refs_0_, bf16[48,1920]{1,0:T(8,128)(2,1)S(1)} %collective-permute-done.5.refs_1_, ...), custom_call_target="tpu_custom_call", output_to_operand_aliasing={{0}: (9, {})} | custom-call | tf_op jit(solution)/shard_map/pallas_call | solution.py:51
  80.5 0.6 collective-permute-start.26
  81.1 1.5 %collective-permute-start.30 = (bf16[72,1024]{1,0:T(8,128)(2,1)S(1)}, bf16[72,1024]{1,0:T(8,128)(2,1)S(1)}, u32[]{:S(2)}, u32[]{:S(2)}) collective-permute-start(bf16[72,1024]{1,0:T(8,128)(2,1)S(1)} %get-tuple-element.37), channel_id=1, source_target_pairs={{0,16},{16,0},{1,17},{17,1},{2,18},{18,2},{3,19},{19,3},{4,20},{20... | collective-permute-start | bytes 442376 | tf_op jit(solution)/shard_map/ppermute | solution.py:17
  82.6 2.6 %collective-permute-done.28.came_ref.came0 = bf16[144,1024]{1,0:T(8,128)(2,1)S(1)} collective-permute-done((bf16[144,1024]{1,0:T(8,128)(2,1)S(1)}, bf16[144,1024]{1,0:T(8,128)(2,1)S(1)}, u32[]{:S(2)}, u32[]{:S(2)}) %collective-permute-start.28) | collective-permute-done | bytes 294944 | tf_op jit(solution)/shard_map/ppermute | solution.py:17
  85.2 0.2 shard_map.85
  85.4 3.4 %collective-permute-start.29 = (bf16[72,1024]{1,0:T(8,128)(2,1)S(1)}, bf16[72,1024]{1,0:T(8,128)(2,1)S(1)}, u32[]{:S(2)}, u32[]{:S(2)}) collective-permute-start(bf16[72,1024]{1,0:T(8,128)(2,1)S(1)} %shard_map.85), channel_id=1, source_target_pairs={{0,8},{1,9},{2,10},{3,11},{4,12},{5,13},{6,14},{7,15},{8,0},{9,1},... | collective-permute-start | bytes 442376 | tf_op jit(solution)/shard_map/ppermute | solution.py:23
  88.9 5.8 %collective-permute-done.26.came_ref.odd1 = bf16[72,1024]{1,0:T(8,128)(2,1)S(1)} collective-permute-done((bf16[72,1024]{1,0:T(8,128)(2,1)S(1)}, bf16[72,1024]{1,0:T(8,128)(2,1)S(1)}, u32[]{:S(2)}, u32[]{:S(2)}) %collective-permute-start.26) | collective-permute-done | bytes 147488 | tf_op jit(solution)/shard_map/ppermute | solution.py:17
  94.7 0.2 shard_map.84
  94.9 3.4 %collective-permute-start.27 = (bf16[72,1024]{1,0:T(8,128)(2,1)S(1)}, bf16[72,1024]{1,0:T(8,128)(2,1)S(1)}, u32[]{:S(2)}, u32[]{:S(2)}) collective-permute-start(bf16[72,1024]{1,0:T(8,128)(2,1)S(1)} %shard_map.84), channel_id=1, source_target_pairs={{0,8},{1,9},{2,10},{3,11},{4,12},{5,13},{6,14},{7,15},{8,0},{9,1},... | collective-permute-start | bytes 442376 | tf_op jit(solution)/shard_map/ppermute | solution.py:23
  98.3 0.0 collective-permute-done.2.far_other_ref
  98.3 8.4 %shard_map.83 = bf16[1,1024,3584]{2,1,0:T(8,128)(2,1)} custom-call(s32[1,16]{1,0:T(1,128)S(1)} %bitcast.6, bf16[288,1024]{1,0:T(8,128)(2,1)S(1)} %get-tuple-element.20.mine_ref, bf16[288,1024]{1,0:T(8,128)(2,1)S(1)} %collective-permute-done.other_ref, bf16[144,1024]{1,0:T(8,128)(2,1)S(1)} %collective-permute-done.1.far_mine_ref, ...), custom_call_target="tpu_custom_call" | custom-call | tf_op jit(solution)/shard_map/pallas_call | solution.py:51
  106.7 0.0 collective-permute-done.30.even1
  106.8 1.9 %shard_map.86.gradient_hbm = bf16[1,2,288,2048]{3,2,1,0:T(8,128)(2,1)} custom-call(s32[1,16]{1,0:T(1,128)S(1)} %bitcast.7, bf16[1,2,288,2048]{3,2,1,0:T(8,128)(2,1)S(1)} %get-tuple-element.32.stored_ref, bf16[144,1024]{1,0:T(8,128)(2,1)S(1)} %get-tuple-element.35.kept_ref.kept0, bf16[144,1024]{1,0:T(8,128)(2,1)S(1)} %collective-permute-done.28.came_ref.came0, ...), custom_call_target="tpu_custom_call" | custom-call | tf_op jit(solution)/shard_map/pallas_call | solution.py:51
  108.7 0.0 collective-permute-done.29.came_ref
  108.7 1.2 %shard_map.87.gradient_hbm = bf16[1,2,288,2048]{3,2,1,0:T(8,128)(2,1)} custom-call(bf16[1,2,288,2048]{3,2,1,0:T(8,128)(2,1)S(1)} %get-tuple-element.32.stored_ref, bf16[72,1024]{1,0:T(8,128)(2,1)S(1)} %collective-permute-done.29.came_ref, bf16[1,2,288,2048]{3,2,1,0:T(8,128)(2,1)} %shard_map.86.gradient_hbm), custom_call_target="tpu_custom_call", output_to_operand_aliasing={{}: (2, {})} | custom-call | tf_op jit(solution)/shard_map/pallas_call | solution.py:51
  109.9 0.0 collective-permute-done.27.came_ref
  109.9 1.2 %shard_map.88 = bf16[1,2,288,2048]{3,2,1,0:T(8,128)(2,1)} custom-call(bf16[1,2,288,2048]{3,2,1,0:T(8,128)(2,1)S(1)} %get-tuple-element.32.stored_ref, bf16[72,1024]{1,0:T(8,128)(2,1)S(1)} %collective-permute-done.27.came_ref, bf16[1,2,288,2048]{3,2,1,0:T(8,128)(2,1)} %shard_map.87.gradient_hbm), custom_call_target="tpu_custom_call", output_to_operand_aliasing={{}: (2, {})} | custom-call | tf_op jit(solution)/shard_map/pallas_call | solution.py:51
  (12 shorter events, 0.0 us)
Async XLA Ops:
  4.5 32.7 %collective-permute-start.1 = (bf16[144,1024]{1,0:T(8,128)(2,1)S(1)}, bf16[144,1024]{1,0:T(8,128)(2,1)S(1)}, u32[]{:S(2)}, u32[]{:S(2)}) collective-permute-start(bf16[144,1024]{1,0:T(8,128)(2,1)S(1)} %get-tuple-element.21), channel_id=1, source_target_pairs={{0,8},{1,9},{2,10},{3,11},{4,12},{5,13},{6,14},{7,15},{8,0},{9,1},... | collective-permute-start | bytes 884744 | tf_op jit(solution)/shard_map/ppermute | solution.py:23
  9.8 24.3 %collective-permute-start.8 = (bf16[48,1792]{1,0:T(8,128)(2,1)S(1)}, bf16[48,1792]{1,0:T(8,128)(2,1)S(1)}, u32[]{:S(2)}, u32[]{:S(2)}) collective-permute-start(bf16[48,1792]{1,0:T(8,128)(2,1)S(1)} %get-tuple-element.23), channel_id=1, source_target_pairs={{0,8},{1,9},{2,10},{3,11},{4,12},{5,13},{6,14},{7,15},{8,0},{9,1},... | collective-permute-start | bytes 516104 | tf_op jit(solution)/shard_map/ppermute | solution.py:17
  9.9 30.4 %collective-permute-start.19 = (bf16[48,3712]{1,0:T(8,128)(2,1)S(1)}, bf16[48,3712]{1,0:T(8,128)(2,1)S(1)}, u32[]{:S(2)}, u32[]{:S(2)}) collective-permute-start(bf16[48,3712]{1,0:T(8,128)(2,1)S(1)} %get-tuple-element.25.refs_0_), channel_id=1, source_target_pairs={{0,4},{1,5},{2,6},{3,7},{4,0},{5,1},{6,2},{7,3},{8,12},{9,13},{10,... | collective-permute-start | bytes 1069064 | tf_op jit(solution)/shard_map/ppermute | solution.py:17
  11.8 25.4 %collective-permute-start.3 = (bf16[48,1920]{1,0:T(8,128)(2,1)S(1)}, bf16[48,1920]{1,0:T(8,128)(2,1)S(1)}, u32[]{:S(2)}, u32[]{:S(2)}) collective-permute-start(bf16[48,1920]{1,0:T(8,128)(2,1)S(1)} %get-tuple-element.22), channel_id=1, source_target_pairs={{0,8},{1,9},{2,10},{3,11},{4,12},{5,13},{6,14},{7,15},{8,0},{9,1},... | collective-permute-start | bytes 552968 | tf_op jit(solution)/shard_map/ppermute | solution.py:17
  14.4 30.6 %collective-permute-start.23 = (bf16[48,3712]{1,0:T(8,128)(2,1)S(1)}, bf16[48,3712]{1,0:T(8,128)(2,1)S(1)}, u32[]{:S(2)}, u32[]{:S(2)}) collective-permute-start(bf16[48,3712]{1,0:T(8,128)(2,1)S(1)} %get-tuple-element.25.refs_0_), channel_id=1, source_target_pairs={{0,2},{1,3},{2,0},{3,1},{4,6},{5,7},{6,4},{7,5},{8,10},{9,11},{10,... | collective-permute-start | bytes 1069064 | tf_op jit(solution)/shard_map/ppermute | solution.py:17
  34.1 5.4 %collective-permute-start.16 = (bf16[48,1792]{1,0:T(8,128)(2,1)S(1)}, bf16[48,1792]{1,0:T(8,128)(2,1)S(1)}, u32[]{:S(2)}, u32[]{:S(2)}) collective-permute-start(bf16[48,1792]{1,0:T(8,128)(2,1)S(1)} %collective-permute-done.8.refs_4_), channel_id=1, source_target_pairs={{0,2},{1,3},{2,0},{3,1},{4,6},{5,7},{6,4},{7,5},{8,10},{9,11},{10,... | collective-permute-start | bytes 516104 | tf_op jit(solution)/shard_map/ppermute | solution.py:17
  37.2 8.5 %collective-permute-start.24 = (bf16[48,3712]{1,0:T(8,128)(2,1)S(1)}, bf16[48,3712]{1,0:T(8,128)(2,1)S(1)}, u32[]{:S(2)}, u32[]{:S(2)}) collective-permute-start(bf16[48,3712]{1,0:T(8,128)(2,1)S(1)} %get-tuple-element.25.refs_0_), channel_id=1, source_target_pairs={{0,1},{1,0},{2,3},{3,2},{4,5},{5,4},{6,7},{7,6},{8,9},{9,8},{10,11... | collective-permute-start | bytes 1069064 | tf_op jit(solution)/shard_map/ppermute | solution.py:17
  37.2 4.6 %collective-permute-start.17 = (bf16[48,1792]{1,0:T(8,128)(2,1)S(1)}, bf16[48,1792]{1,0:T(8,128)(2,1)S(1)}, u32[]{:S(2)}, u32[]{:S(2)}) collective-permute-start(bf16[48,1792]{1,0:T(8,128)(2,1)S(1)} %collective-permute-done.8.refs_4_), channel_id=1, source_target_pairs={{0,1},{1,0},{2,3},{3,2},{4,5},{5,4},{6,7},{7,6},{8,9},{9,8},{10,11... | collective-permute-start | bytes 516104 | tf_op jit(solution)/shard_map/ppermute | solution.py:17
  39.5 5.4 %collective-permute-start.9 = (bf16[48,1792]{1,0:T(8,128)(2,1)S(1)}, bf16[48,1792]{1,0:T(8,128)(2,1)S(1)}, u32[]{:S(2)}, u32[]{:S(2)}) collective-permute-start(bf16[48,1792]{1,0:T(8,128)(2,1)S(1)} %collective-permute-done.8.refs_4_), channel_id=1, source_target_pairs={{0,4},{1,5},{2,6},{3,7},{4,0},{5,1},{6,2},{7,3},{8,12},{9,13},{10,... | collective-permute-start | bytes 516104 | tf_op jit(solution)/shard_map/ppermute | solution.py:17
  40.3 15.0 %collective-permute-start.20 = (bf16[48,3712]{1,0:T(8,128)(2,1)S(1)}, bf16[48,3712]{1,0:T(8,128)(2,1)S(1)}, u32[]{:S(2)}, u32[]{:S(2)}) collective-permute-start(bf16[48,3712]{1,0:T(8,128)(2,1)S(1)} %collective-permute-done.19.refs_0_), channel_id=1, source_target_pairs={{0,2},{1,3},{2,0},{3,1},{4,6},{5,7},{6,4},{7,5},{8,10},{9,11},{10,... | collective-permute-start | bytes 1069064 | tf_op jit(solution)/shard_map/ppermute | solution.py:17
  41.8 11.5 %collective-permute-start.13 = (bf16[48,1920]{1,0:T(8,128)(2,1)S(1)}, bf16[48,1920]{1,0:T(8,128)(2,1)S(1)}, u32[]{:S(2)}, u32[]{:S(2)}) collective-permute-start(bf16[48,1920]{1,0:T(8,128)(2,1)S(1)} %collective-permute-done.3.refs_0_), channel_id=1, source_target_pairs={{0,2},{1,3},{2,0},{3,1},{4,6},{5,7},{6,4},{7,5},{8,10},{9,11},{10,... | collective-permute-start | bytes 552968 | tf_op jit(solution)/shard_map/ppermute | solution.py:17
  44.9 9.9 %collective-permute-start.14 = (bf16[48,1920]{1,0:T(8,128)(2,1)S(1)}, bf16[48,1920]{1,0:T(8,128)(2,1)S(1)}, u32[]{:S(2)}, u32[]{:S(2)}) collective-permute-start(bf16[48,1920]{1,0:T(8,128)(2,1)S(1)} %collective-permute-done.3.refs_0_), channel_id=1, source_target_pairs={{0,1},{1,0},{2,3},{3,2},{4,5},{5,4},{6,7},{7,6},{8,9},{9,8},{10,11... | collective-permute-start | bytes 552968 | tf_op jit(solution)/shard_map/ppermute | solution.py:17
  44.9 9.9 %collective-permute-start.4 = (bf16[48,1920]{1,0:T(8,128)(2,1)S(1)}, bf16[48,1920]{1,0:T(8,128)(2,1)S(1)}, u32[]{:S(2)}, u32[]{:S(2)}) collective-permute-start(bf16[48,1920]{1,0:T(8,128)(2,1)S(1)} %collective-permute-done.3.refs_0_), channel_id=1, source_target_pairs={{0,4},{1,5},{2,6},{3,7},{4,0},{5,1},{6,2},{7,3},{8,12},{9,13},{10,... | collective-permute-start | bytes 552968 | tf_op jit(solution)/shard_map/ppermute | solution.py:17
  45.7 9.6 %collective-permute-start.18 = (bf16[48,1792]{1,0:T(8,128)(2,1)S(1)}, bf16[48,1792]{1,0:T(8,128)(2,1)S(1)}, u32[]{:S(2)}, u32[]{:S(2)}) collective-permute-start(bf16[48,1792]{1,0:T(8,128)(2,1)S(1)} %collective-permute-done.16.refs_5_), channel_id=1, source_target_pairs={{0,1},{1,0},{2,3},{3,2},{4,5},{5,4},{6,7},{7,6},{8,9},{9,8},{10,11... | collective-permute-start | bytes 516104 | tf_op jit(solution)/shard_map/ppermute | solution.py:17
  53.3 5.6 %collective-permute-start.10 = (bf16[48,1792]{1,0:T(8,128)(2,1)S(1)}, bf16[48,1792]{1,0:T(8,128)(2,1)S(1)}, u32[]{:S(2)}, u32[]{:S(2)}) collective-permute-start(bf16[48,1792]{1,0:T(8,128)(2,1)S(1)} %collective-permute-done.9.refs_4_), channel_id=1, source_target_pairs={{0,2},{1,3},{2,0},{3,1},{4,6},{5,7},{6,4},{7,5},{8,10},{9,11},{10,... | collective-permute-start | bytes 516104 | tf_op jit(solution)/shard_map/ppermute | solution.py:17
  54.8 11.2 %collective-permute-start.25 = (bf16[48,3712]{1,0:T(8,128)(2,1)S(1)}, bf16[48,3712]{1,0:T(8,128)(2,1)S(1)}, u32[]{:S(2)}, u32[]{:S(2)}) collective-permute-start(bf16[48,3712]{1,0:T(8,128)(2,1)S(1)} %collective-permute-done.23.refs_1_), channel_id=1, source_target_pairs={{0,1},{1,0},{2,3},{3,2},{4,5},{5,4},{6,7},{7,6},{8,9},{9,8},{10,11... | collective-permute-start | bytes 1069064 | tf_op jit(solution)/shard_map/ppermute | solution.py:17
  54.8 11.2 %collective-permute-start.21 = (bf16[48,3712]{1,0:T(8,128)(2,1)S(1)}, bf16[48,3712]{1,0:T(8,128)(2,1)S(1)}, u32[]{:S(2)}, u32[]{:S(2)}) collective-permute-start(bf16[48,3712]{1,0:T(8,128)(2,1)S(1)} %collective-permute-done.19.refs_0_), channel_id=1, source_target_pairs={{0,1},{1,0},{2,3},{3,2},{4,5},{5,4},{6,7},{7,6},{8,9},{9,8},{10,11... | collective-permute-start | bytes 1069064 | tf_op jit(solution)/shard_map/ppermute | solution.py:17
  55.3 11.2 %collective-permute-start.22 = (bf16[48,3712]{1,0:T(8,128)(2,1)S(1)}, bf16[48,3712]{1,0:T(8,128)(2,1)S(1)}, u32[]{:S(2)}, u32[]{:S(2)}) collective-permute-start(bf16[48,3712]{1,0:T(8,128)(2,1)S(1)} %collective-permute-done.20.refs_1_), channel_id=1, source_target_pairs={{0,1},{1,0},{2,3},{3,2},{4,5},{5,4},{6,7},{7,6},{8,9},{9,8},{10,11... | collective-permute-start | bytes 1069064 | tf_op jit(solution)/shard_map/ppermute | solution.py:17
  55.4 5.4 %collective-permute-start.15 = (bf16[48,1920]{1,0:T(8,128)(2,1)S(1)}, bf16[48,1920]{1,0:T(8,128)(2,1)S(1)}, u32[]{:S(2)}, u32[]{:S(2)}) collective-permute-start(bf16[48,1920]{1,0:T(8,128)(2,1)S(1)} %collective-permute-done.13.refs_1_), channel_id=1, source_target_pairs={{0,1},{1,0},{2,3},{3,2},{4,5},{5,4},{6,7},{7,6},{8,9},{9,8},{10,11... | collective-permute-start | bytes 552968 | tf_op jit(solution)/shard_map/ppermute | solution.py:17
  58.9 5.5 %collective-permute-start.5 = (bf16[48,1920]{1,0:T(8,128)(2,1)S(1)}, bf16[48,1920]{1,0:T(8,128)(2,1)S(1)}, u32[]{:S(2)}, u32[]{:S(2)}) collective-permute-start(bf16[48,1920]{1,0:T(8,128)(2,1)S(1)} %collective-permute-done.4.refs_0_), channel_id=1, source_target_pairs={{0,2},{1,3},{2,0},{3,1},{4,6},{5,7},{6,4},{7,5},{8,10},{9,11},{10,... | collective-permute-start | bytes 552968 | tf_op jit(solution)/shard_map/ppermute | solution.py:17
  60.8 14.5 %collective-permute-start.11 = (bf16[48,1792]{1,0:T(8,128)(2,1)S(1)}, bf16[48,1792]{1,0:T(8,128)(2,1)S(1)}, u32[]{:S(2)}, u32[]{:S(2)}) collective-permute-start(bf16[48,1792]{1,0:T(8,128)(2,1)S(1)} %collective-permute-done.9.refs_4_), channel_id=1, source_target_pairs={{0,1},{1,0},{2,3},{3,2},{4,5},{5,4},{6,7},{7,6},{8,9},{9,8},{10,11... | collective-permute-start | bytes 516104 | tf_op jit(solution)/shard_map/ppermute | solution.py:17
  64.4 33.9 %collective-permute-start = (bf16[288,1024]{1,0:T(8,128)(2,1)S(1)}, bf16[288,1024]{1,0:T(8,128)(2,1)S(1)}, u32[]{:S(2)}, u32[]{:S(2)}) collective-permute-start(bf16[288,1024]{1,0:T(8,128)(2,1)S(1)} %get-tuple-element.20.mine_ref), channel_id=1, source_target_pairs={{0,16},{16,0},{1,17},{17,1},{2,18},{18,2},{3,19},{19,3},{4,20},{20... | collective-permute-start | bytes 1769480 | tf_op jit(solution)/shard_map/ppermute | solution.py:17
  66.0 9.9 %collective-permute-start.6 = (bf16[48,1920]{1,0:T(8,128)(2,1)S(1)}, bf16[48,1920]{1,0:T(8,128)(2,1)S(1)}, u32[]{:S(2)}, u32[]{:S(2)}) collective-permute-start(bf16[48,1920]{1,0:T(8,128)(2,1)S(1)} %collective-permute-done.4.refs_0_), channel_id=1, source_target_pairs={{0,1},{1,0},{2,3},{3,2},{4,5},{5,4},{6,7},{7,6},{8,9},{9,8},{10,11... | collective-permute-start | bytes 552968 | tf_op jit(solution)/shard_map/ppermute | solution.py:17
  66.0 11.4 %collective-permute-start.7 = (bf16[48,1920]{1,0:T(8,128)(2,1)S(1)}, bf16[48,1920]{1,0:T(8,128)(2,1)S(1)}, u32[]{:S(2)}, u32[]{:S(2)}) collective-permute-start(bf16[48,1920]{1,0:T(8,128)(2,1)S(1)} %collective-permute-done.5.refs_1_), channel_id=1, source_target_pairs={{0,1},{1,0},{2,3},{3,2},{4,5},{5,4},{6,7},{7,6},{8,9},{9,8},{10,11... | collective-permute-start | bytes 552968 | tf_op jit(solution)/shard_map/ppermute | solution.py:17
  66.5 10.9 %collective-permute-start.12 = (bf16[48,1792]{1,0:T(8,128)(2,1)S(1)}, bf16[48,1792]{1,0:T(8,128)(2,1)S(1)}, u32[]{:S(2)}, u32[]{:S(2)}) collective-permute-start(bf16[48,1792]{1,0:T(8,128)(2,1)S(1)} %collective-permute-done.10.refs_5_), channel_id=1, source_target_pairs={{0,1},{1,0},{2,3},{3,2},{4,5},{5,4},{6,7},{7,6},{8,9},{9,8},{10,11... | collective-permute-start | bytes 516104 | tf_op jit(solution)/shard_map/ppermute | solution.py:17
  75.3 9.9 %collective-permute-start.28 = (bf16[144,1024]{1,0:T(8,128)(2,1)S(1)}, bf16[144,1024]{1,0:T(8,128)(2,1)S(1)}, u32[]{:S(2)}, u32[]{:S(2)}) collective-permute-start(bf16[144,1024]{1,0:T(8,128)(2,1)S(1)} %get-tuple-element.36), channel_id=1, source_target_pairs={{0,16},{16,0},{1,17},{17,1},{2,18},{18,2},{3,19},{19,3},{4,20},{20... | collective-permute-start | bytes 884744 | tf_op jit(solution)/shard_map/ppermute | solution.py:17
  75.8 22.5 %collective-permute-start.2 = (bf16[144,1024]{1,0:T(8,128)(2,1)S(1)}, bf16[144,1024]{1,0:T(8,128)(2,1)S(1)}, u32[]{:S(2)}, u32[]{:S(2)}) collective-permute-start(bf16[144,1024]{1,0:T(8,128)(2,1)S(1)} %collective-permute-done.1.far_mine_ref), channel_id=1, source_target_pairs={{0,16},{16,0},{1,17},{17,1},{2,18},{18,2},{3,19},{19,3},{4,20},{20... | collective-permute-start | bytes 884744 | tf_op jit(solution)/shard_map/ppermute | solution.py:17
  77.4 7.8 %copy-start = (s32[16]{0:T(128)S(1)}, s32[16]{0:T(128)}, u32[]{:S(2)}) copy-start(s32[16]{0:T(128)} %param.9) | copy-start | bytes 196
  80.5 14.2 %collective-permute-start.26 = (bf16[72,1024]{1,0:T(8,128)(2,1)S(1)}, bf16[72,1024]{1,0:T(8,128)(2,1)S(1)}, u32[]{:S(2)}, u32[]{:S(2)}) collective-permute-start(bf16[72,1024]{1,0:T(8,128)(2,1)S(1)} %get-tuple-element.34), channel_id=1, source_target_pairs={{0,16},{16,0},{1,17},{17,1},{2,18},{18,2},{3,19},{19,3},{4,20},{20... | collective-permute-start | bytes 442376 | tf_op jit(solution)/shard_map/ppermute | solution.py:17
  81.1 25.7 %collective-permute-start.30 = (bf16[72,1024]{1,0:T(8,128)(2,1)S(1)}, bf16[72,1024]{1,0:T(8,128)(2,1)S(1)}, u32[]{:S(2)}, u32[]{:S(2)}) collective-permute-start(bf16[72,1024]{1,0:T(8,128)(2,1)S(1)} %get-tuple-element.37), channel_id=1, source_target_pairs={{0,16},{16,0},{1,17},{17,1},{2,18},{18,2},{3,19},{19,3},{4,20},{20... | collective-permute-start | bytes 442376 | tf_op jit(solution)/shard_map/ppermute | solution.py:17
  85.4 23.3 %collective-permute-start.29 = (bf16[72,1024]{1,0:T(8,128)(2,1)S(1)}, bf16[72,1024]{1,0:T(8,128)(2,1)S(1)}, u32[]{:S(2)}, u32[]{:S(2)}) collective-permute-start(bf16[72,1024]{1,0:T(8,128)(2,1)S(1)} %shard_map.85), channel_id=1, source_target_pairs={{0,8},{1,9},{2,10},{3,11},{4,12},{5,13},{6,14},{7,15},{8,0},{9,1},... | collective-permute-start | bytes 442376 | tf_op jit(solution)/shard_map/ppermute | solution.py:23
  94.9 15.0 %collective-permute-start.27 = (bf16[72,1024]{1,0:T(8,128)(2,1)S(1)}, bf16[72,1024]{1,0:T(8,128)(2,1)S(1)}, u32[]{:S(2)}, u32[]{:S(2)}) collective-permute-start(bf16[72,1024]{1,0:T(8,128)(2,1)S(1)} %shard_map.84), channel_id=1, source_target_pairs={{0,8},{1,9},{2,10},{3,11},{4,12},{5,13},{6,14},{7,15},{8,0},{9,1},... | collective-permute-start | bytes 442376 | tf_op jit(solution)/shard_map/ppermute | solution.py:23
